TPU v7x, 128 devices: a whole 4x4x4 slice. The times are simulated.
128 devices in a mesh: grp: 8 (over z, core), mem: 16 (over y, x).
Axes of the slice: x: 4, y: 4, z: 4, core: 2. Of those that a mesh axis runs over, the one named last changes fastest.
Arguments:
- forcing: float32 [3, 1024, 4096], P(None, ('grp', 'mem')), may hold values from -6 to 6
- viscosity: float32 [1024, 4096], P(('grp', 'mem')), may hold values from 0.1 to 10
- refinement: int32 [1024], P(('grp', 'mem')), may hold values from 0 to 1
- face_owner: int32 [4096, 1], P(('grp', 'mem')), may hold values from 0 to 15; in each aligned block of 32 rows (0 to 31, 32 to 63, ...) at most 4 rows name the same one
- face_block: int32 [1024, 4], P(('grp', 'mem')), may hold values from 0 to 7
- plane_block: int32 [1024, 2], P(('grp', 'mem')), may hold values from 0 to 7
- hanging: int32 [1024, 6], P(('grp', 'mem')), may hold values 0 or 1
- coarse_solver: float32 [8, 384, 384], P('grp', 'mem'), may hold values from -0.3125 to 0.3125
Outputs:
- velocity: float32 [3, 1024, 4096], P(None, ('grp', 'mem'))
- residual: float32 [3, 1024, 4096], P(None, ('grp', 'mem'))
Inputs may be any that keep to these rules, and one draw needn't show every extreme that they name: `face_owner`: among the 32 rows of one device no member appears more than 4 times, and some member appears exactly 4 times.
All inputs are finite; a program needn't handle non-finite values. No bound on the sum of `hanging` on one device may be relied on, other than what follows from the above.
Results may differ from a plain program's by a relative error of at most 0.0001.
Values sent between devices are 32-bit elements; how exact they have to be, the bound alone decides.
A program may use at most 64 MiB of HBM per device.

v0:
```python
import math
import jax
import jax.numpy as jnp
from jax import lax
from jax.sharding import PartitionSpec as P

EDGE = 16
DEG = 3
CELLS = 4096
FACE = 256
MASS_TERM = 1.0
LOWER_BOUND = 0.25
UPPER_BOUND = 2.0
HIGHEST = lax.Precision.HIGHEST


def shifted_2(block, axis, distance):
    devices = range(lax.axis_size(axis))
    route = [(i - distance, i) for i in devices if i - distance in devices]
    return lax.ppermute(block, axis, route)


def coarsen(plane_vals):
    leading = plane_vals.shape[:-1]
    squares = plane_vals.reshape(leading + (EDGE // 2, 2, EDGE // 2, 2))
    average = jnp.mean(squares, axis=(-3, -1), keepdims=True)
    return jnp.broadcast_to(average, squares.shape).reshape(leading + (FACE,))


def tables():
    lanes = jnp.arange(FACE, dtype=jnp.int32)
    lane_k = lanes % EDGE
    lane_j = lanes // EDGE
    sources = [lanes - 1, lanes + 1, lanes - EDGE, lanes + EDGE]
    valid = [lane_k > 0, lane_k < EDGE - 1, lane_j > 0, lane_j < EDGE - 1]
    shift_mat = jnp.concatenate(
        [
            ((lanes[:, None] == sources[d][None, :]) & valid[d][None, :]).astype(jnp.float32)
            for d in range(4)
        ],
        axis=1,
    )
    places = jnp.arange(EDGE, dtype=jnp.int32)
    picks = [places * EDGE, places * EDGE + EDGE - 1, places, (EDGE - 1) * EDGE + places]
    pick_mats = [(lanes[:, None] == picks[d][None, :]).astype(jnp.float32) for d in range(4)]
    return (shift_mat, pick_mats)


def far_faces(upper_planes, lower_planes, plane_block):
    arrived = []
    for by_step, outgoing in ((1, upper_planes), (-1, lower_planes)):
        arrived.append(shifted_2(outgoing, "grp", by_step))
    lower_ghost = jnp.take(arrived[0], plane_block[:, 0], axis=1)
    upper_ghost = jnp.take(arrived[1], plane_block[:, 1], axis=1)
    return (lower_ghost, upper_ghost)


def local(
    forcing, viscosity, refinement, face_owner, face_block, plane_block, hanging, coarse_solver
):
    blocks_here = forcing.shape[1]
    shift_mat, pick_mats = tables()
    pick_all = jnp.concatenate(pick_mats, axis=1)
    forcing_cube = forcing.reshape(3, blocks_here, EDGE, FACE)
    effective = (
        viscosity.reshape(blocks_here, EDGE, FACE)
        * jnp.exp2(-refinement.astype(jnp.float32))[:, None, None]
    )
    owners = face_owner[:, 0]
    opposite = jnp.array([1, 0, 3, 2], jnp.int32)
    wanted = (face_block * 4 + opposite[None, :]).reshape(-1)

    def near_faces(face_rows):
        gathered = lax.all_gather(face_rows, "mem", axis=0, tiled=True)
        return gathered[owners * (4 * blocks_here) + wanted]

    def ghost_set(stacked):
        channels = stacked.shape[0]
        picked = jnp.einsum("cbil,lm->cbim", stacked, pick_all, precision=HIGHEST)
        face_rows = (
            picked.reshape(channels, blocks_here, EDGE, 4, EDGE)
            .transpose(1, 3, 0, 2, 4)
            .reshape(blocks_here * 4, channels * FACE)
        )
        ghost_rows = near_faces(face_rows).reshape(blocks_here, 4, channels, FACE)
        result = [ghost_rows[:, direction].transpose(1, 0, 2) for direction in range(4)]
        lower_ghost, upper_ghost = far_faces(
            stacked[:, :, EDGE - 1, :], stacked[:, :, 0, :], plane_block
        )
        result.append(lower_ghost)
        result.append(upper_ghost)
        return [
            jnp.where(
                hanging[:, direction][None, :, None] == 1,
                coarsen(result[direction]),
                result[direction],
            )
            for direction in range(6)
        ]

    def beside(values, ghosts):
        channels = values.shape[0]
        shifted = jnp.einsum("cbil,lm->cbim", values, shift_mat, precision=HIGHEST)
        nearby = []
        for direction in range(4):
            placed = jnp.einsum(
                "cbim,lm->cbil",
                ghosts[direction].reshape(channels, blocks_here, EDGE, EDGE),
                pick_mats[direction],
                precision=HIGHEST,
            )
            nearby.append(shifted[..., direction * FACE : (direction + 1) * FACE] + placed)
        nearby.append(jnp.concatenate([ghosts[4][:, :, None, :], values[:, :, :-1, :]], axis=2))
        nearby.append(jnp.concatenate([values[:, :, 1:, :], ghosts[5][:, :, None, :]], axis=2))
        return nearby

    nearby_eff = beside(effective[None], ghost_set(effective[None]))
    weights = [0.5 * (effective + nearby_eff[direction][0]) for direction in range(6)]
    diagonal = MASS_TERM * effective
    for direction in range(6):
        diagonal = diagonal + weights[direction]

    def operate(values):
        nearby = beside(values, ghost_set(values))
        applied = diagonal * values
        for direction in range(6):
            applied = applied - weights[direction] * nearby[direction]
        return applied

    midpoint = 0.5 * (UPPER_BOUND + LOWER_BOUND)
    half_width = 0.5 * (UPPER_BOUND - LOWER_BOUND)
    sigma_ratio = midpoint / half_width

    def smooth(solution, residual):
        rho_now = 1.0 / sigma_ratio
        step_dir = residual / (diagonal * midpoint)
        for sweep_index in range(DEG):
            solution = solution + step_dir
            residual = residual - operate(step_dir)
            if sweep_index < DEG - 1:
                rho_next = 1.0 / (2.0 * sigma_ratio - rho_now)
                step_dir = rho_next * rho_now * step_dir + 2.0 * rho_next / half_width * (
                    residual / diagonal
                )
                rho_now = rho_next
        return (solution, residual)

    solution, residual = smooth(jnp.zeros_like(forcing_cube), forcing_cube)
    coarse_local = (jnp.sum(residual, axis=(2, 3)) / math.sqrt(CELLS)).T.reshape(-1)
    rows_here = coarse_solver[0]
    correction = jnp.dot(
        rows_here,
        lax.all_gather(coarse_local, "mem", axis=0, tiled=True),
        precision=HIGHEST,
        preferred_element_type=jnp.float32,
    )
    lifted = jnp.broadcast_to(
        correction.reshape(blocks_here, 3).T[:, :, None, None], forcing_cube.shape
    )
    solution = solution + lifted
    residual = residual - operate(lifted)
    solution, residual = smooth(solution, residual)
    return (solution.reshape(forcing.shape), residual.reshape(forcing.shape))


def solution(mesh):
    in_specs = (
        P(None, ("grp", "mem"), None),
        P(("grp", "mem"), None),
        P(("grp", "mem")),
        P(("grp", "mem"), None),
        P(("grp", "mem"), None),
        P(("grp", "mem"), None),
        P(("grp", "mem"), None),
        P("grp", "mem", None),
    )
    out_specs = (P(None, ("grp", "mem"), None), P(None, ("grp", "mem"), None))
    return jax.shard_map(local, mesh=mesh, in_specs=in_specs, out_specs=out_specs, check_vma=False)
```

profile of v0, /device:TPU:0, one launch (start us, length us, event | category | flops | bytes accessed | tf_op | source)
XLA Modules:
  0.0 607.3 jit_solution(15840290535157774675)
XLA Ops:
  14.4 24.8 %all_gather.27 = f32[512,256]{1,0:T(8,128)S(1)} all-gather(f32[32,256]{1,0:T(8,128)S(1)} %reshape.1007), channel_id=1, replica_groups=mesh['grp'=8,'mem'=16] {'mem'}, dimensions={0}, use_global_device_ids=true | all-gather | bytes 557056 | tf_op jit(solution)/shard_map/all_gather | solution.py:74
  51.9 1.6 collective-permute-start.3
  71.7 24.8 %all-gather.8.cloned.1.call-done = f32[512,768]{1,0:T(8,128)} async-done(((f32[32,768]{1,0:T(8,128)}), f32[512,768]{1,0:T(8,128)}) %all-gather.8.cloned.1.call-update) | async-done | bytes 1572880 | tf_op jit(solution)/shard_map/all_gather | solution.py:74
  96.5 2.2 gather_fusion.1
  127.2 1.5 collective-permute-start.5
  129.4 2.1 gather_fusion.12
  132.9 1.6 copy.570
  134.5 2.0 reduce_sum.457
  138.3 1.7 copy.571
  142.9 2.0 gather_fusion.13
  146.3 1.6 copy.575
  148.0 1.9 reduce_sum.458
  151.7 1.7 copy.576
  154.9 11.5 %all-gather.10.cloned.1.call-done = f32[512,768]{1,0:T(8,128)} async-done(((f32[32,768]{1,0:T(8,128)}), f32[512,768]{1,0:T(8,128)}) %all-gather.10.cloned.1.call-update) | async-done | bytes 1572880 | tf_op jit(solution)/shard_map/all_gather | solution.py:74
  166.4 2.8 gather_fusion.2
  169.3 1.6 reshape.1032
  172.3 1.7 copy.553
  174.0 2.0 reduce_sum.453
  177.7 1.8 copy.554
  179.5 1.7 copy.557
  181.1 2.0 reduce_sum.454
  184.9 1.8 copy.558
  186.6 1.7 copy.561
  188.3 2.0 reduce_sum.455
  192.0 1.8 copy.562
  193.8 1.7 copy.565
  195.5 1.9 reduce_sum.456
  199.2 1.8 copy.566
  200.9 1.6 broadcast_select_fusion.9
  203.1 1.5 reshape.1035
  206.0 1.5 reshape.1038
  211.8 1.5 reshape.1044
  216.0 1.5 multiply_add_fusion.2
  226.1 2.0 fusion.97
  229.0 1.7 collective-permute-start.7
  236.2 28.4 %all-gather.12.cloned.1.call-done = f32[512,768]{1,0:T(8,128)} async-done(((f32[32,768]{1,0:T(8,128)}), f32[512,768]{1,0:T(8,128)}) %all-gather.12.cloned.1.call-update) | async-done | bytes 1572880 | tf_op jit(solution)/shard_map/all_gather | solution.py:74
  264.5 2.2 gather_fusion.3
  281.1 38.1 %all-reduce = f32[384]{0:T(512)S(1)} all-reduce(f32[384]{0:T(512)S(1)} %dynamic-update-slice), channel_id=1, replica_groups=mesh['grp'=8,'mem'=16] {'mem'}, use_global_device_ids=true, to_apply=%add | all-reduce | flops 384 | bytes 3072
  321.0 2.1 reshape.1069
  324.6 2.0 fusion.95
  326.6 1.6 collective-permute-start.9
  333.9 29.4 %all-gather.14.cloned.1.call-done = f32[512,768]{1,0:T(8,128)} async-done(((f32[32,768]{1,0:T(8,128)}), f32[512,768]{1,0:T(8,128)}) %all-gather.14.cloned.1.call-update) | async-done | bytes 1572880 | tf_op jit(solution)/shard_map/all_gather | solution.py:74
  363.2 2.2 gather_fusion.4
  380.8 2.0 fusion.93
  401.3 21.2 %all-gather.16.cloned.1.call-done = f32[512,768]{1,0:T(8,128)} async-done(((f32[32,768]{1,0:T(8,128)}), f32[512,768]{1,0:T(8,128)}) %all-gather.16.cloned.1.call-update) | async-done | bytes 1572880 | tf_op jit(solution)/shard_map/all_gather | solution.py:74
  422.5 2.2 gather_fusion.5
  450.0 2.1 copy.658
  452.1 2.1 reshape.1107
  455.6 2.0 fusion.91
  459.2 1.5 collective-permute-start.13
  476.4 21.0 %all-gather.18.cloned.1.call-done = f32[512,768]{1,0:T(8,128)} async-done(((f32[32,768]{1,0:T(8,128)}), f32[512,768]{1,0:T(8,128)}) %all-gather.18.cloned.1.call-update) | async-done | bytes 1572880 | tf_op jit(solution)/shard_map/all_gather | solution.py:74
  497.3 2.2 gather_fusion.6
  522.1 1.6 add_add_fusion
  526.1 1.9 collective-permute-start.14
  528.5 1.6 collective-permute-start.15
  531.8 1.8 reshape.1125
  546.6 22.0 %all-gather.20.cloned.1.call-done = f32[512,768]{1,0:T(8,128)} async-done(((f32[32,768]{1,0:T(8,128)}), f32[512,768]{1,0:T(8,128)}) %all-gather.20.cloned.1.call-update) | async-done | bytes 1572880 | tf_op jit(solution)/shard_map/all_gather | solution.py:74
  568.5 2.2 gather_fusion.7
  575.7 1.7 copy.691
  579.6 1.8 copy.692
  581.4 1.7 copy.695
  585.3 1.8 copy.696
  587.1 1.7 copy.699
  590.9 1.8 copy.700
  (836 shorter events, 266.1 us)
Async XLA Ops:
  7.2 32.1 %copy-start.144 = (s32[4]{0:T(128)S(1)}, s32[4]{0:T(128)}, u32[]{:S(2)}) copy-start(s32[4]{0:T(128)} %constant.145.clone) | copy-start | bytes 52
  7.2 32.1 %copy-start.142 = (s32[8,4]{0,1:T(4,128)S(1)}, s32[8,4]{0,1:T(4,128)}, u32[]{:S(2)}) copy-start(s32[8,4]{0,1:T(4,128)} %param.17) | copy-start | bytes 388
  7.2 32.3 %copy-start.145 = (s32[32,1]{0,1:T(1,128)S(1)}, s32[32,1]{0,1:T(1,128)}, u32[]{:S(2)}) copy-start(s32[32,1]{0,1:T(1,128)} %param.16) | copy-start | bytes 388
  7.2 89.3 %all-gather.8.cloned.1.call-start = ((), (), s32[]{:S(2)}) async-start(), calls=%async_computation | async-start | bytes 1671168 | tf_op jit(solution)/shard_map/all_gather | solution.py:74
  7.9 39.2 %copy-start.140 = (f32[8]{0:T(128)}, f32[8]{0:T(128)S(1)}, u32[]{:S(2)}) copy-start(f32[8]{0:T(128)S(1)} %multiply_exponential_fusion) | copy-start | bytes 100
  8.9 35.8 %collective-permute-start = (f32[1,8,256]{2,0,1:T(1,128)S(1)}, f32[1,8,256]{2,0,1:T(1,128)S(1)}, u32[]{:S(2)}, u32[]{:S(2)}) collective-permute-start(f32[1,8,256]{2,0,1:T(1,128)S(1)} %get-tuple-element.104), channel_id=1, source_target_pairs={{0,16},{16,32},{32,48},{48,64},{64,80},{80,96},{96,112},{1,17},{17... | collective-permute-start | bytes 24584 | tf_op jit(solution)/shard_map/ppermute | solution.py:20
  10.2 35.6 %collective-permute-start.1 = (f32[1,8,256]{2,0,1:T(1,128)S(1)}, f32[1,8,256]{2,0,1:T(1,128)S(1)}, u32[]{:S(2)}, u32[]{:S(2)}) collective-permute-start(f32[1,8,256]{2,0,1:T(1,128)S(1)} %get-tuple-element.105), channel_id=1, source_target_pairs={{16,0},{32,16},{48,32},{64,48},{80,64},{96,80},{112,96},{17,1},{33... | collective-permute-start | bytes 24584 | tf_op jit(solution)/shard_map/ppermute | solution.py:20
  11.5 32.2 %copy-start.129 = (s32[16]{0:T(128)}, s32[16]{0:T(128)S(1)}, u32[]{:S(2)}) copy-start(s32[16]{0:T(128)S(1)} %iota_add_fusion.4) | copy-start | bytes 196
  11.5 31.4 %copy-start.122 = (s32[16]{0:T(128)}, s32[16]{0:T(128)S(1)}, u32[]{:S(2)}) copy-start(s32[16]{0:T(128)S(1)} %broadcast_add_fusion) | copy-start | bytes 196
  11.6 31.1 %copy-start.127 = (s32[16]{0:T(128)}, s32[16]{0:T(128)S(1)}, u32[]{:S(2)}) copy-start(s32[16]{0:T(128)S(1)} %iota_multiply_fusion) | copy-start | bytes 196
  11.6 29.4 %copy-start.70 = (s32[8,6]{1,0:T(8,128)S(1)}, s32[8,6]{1,0:T(8,128)}, u32[]{:S(2)}) copy-start(s32[8,6]{1,0:T(8,128)} %param.19) | copy-start | bytes 580
  41.3 5.5 copy-start.114
  41.4 5.6 copy-start.118
  44.7 3.3 copy-start.71
  44.7 3.3 copy-start.77
  49.7 116.8 %all-gather.10.cloned.1.call-start = ((), (), s32[]{:S(2)}) async-start(), calls=%async_computation.1 | async-start | bytes 1671168 | tf_op jit(solution)/shard_map/all_gather | solution.py:74
  49.9 5.5 collective-permute-start.2
  51.8 3.4 copy-start.7
  51.8 3.5 copy-start.45
  51.8 3.5 copy-start.46
  51.8 3.5 copy-start.96
  51.8 3.5 copy-start.98
  51.8 3.5 copy-start.141
  51.9 11.4 %collective-permute-start.3 = (f32[3,8,256]{2,1,0:T(8,128)}, f32[3,8,256]{2,1,0:T(8,128)}, u32[]{:S(2)}, u32[]{:S(2)}) collective-permute-start(f32[3,8,256]{2,1,0:T(8,128)} %bitcast.760), channel_id=1, source_target_pairs={{16,0},{32,16},{48,32},{64,48},{80,64},{96,80},{112,96},{17,1},{33... | collective-permute-start | bytes 73736 | tf_op jit(solution)/shard_map/ppermute | solution.py:20
  123.3 141.2 %all-gather.12.cloned.1.call-start = ((), (), s32[]{:S(2)}) async-start(), calls=%async_computation.2 | async-start | bytes 1671168 | tf_op jit(solution)/shard_map/all_gather | solution.py:74
  123.4 5.3 collective-permute-start.4
  125.6 89.6 %copy-start.1 = (f32[3,8,16,1024]{3,2,1,0:T(8,128)}, f32[3,8,16,1024]{3,2,1,0:T(8,128)S(1)}, u32[]{:S(2)}) copy-start(f32[3,8,16,1024]{3,2,1,0:T(8,128)S(1)} %fusion.99) | copy-start | bytes 4718596
  127.2 14.3 %collective-permute-start.5 = (f32[3,8,256]{2,1,0:T(8,128)}, f32[3,8,256]{2,1,0:T(8,128)}, u32[]{:S(2)}, u32[]{:S(2)}) collective-permute-start(f32[3,8,256]{2,1,0:T(8,128)} %bitcast.758), channel_id=1, source_target_pairs={{16,0},{32,16},{48,32},{64,48},{80,64},{96,80},{112,96},{17,1},{33... | collective-permute-start | bytes 73736 | tf_op jit(solution)/shard_map/ppermute | solution.py:20
  221.4 141.8 %all-gather.14.cloned.1.call-start = ((), (), s32[]{:S(2)}) async-start(), calls=%async_computation.3 | async-start | bytes 1671168 | tf_op jit(solution)/shard_map/all_gather | solution.py:74
  224.8 6.7 %copy-start.72 = (pred[8]{0:T(512)(128)(4,1)S(1)}, pred[8]{0:T(512)(128)(4,1)}, u32[]{:S(2)}) copy-start(pred[8]{0:T(512)(128)(4,1)} %copy-done.71) | copy-start | bytes 28
  224.8 6.0 collective-permute-start.6
  228.1 4.3 copy-start.115
  229.0 5.6 copy-start.78
  229.0 4.9 collective-permute-start.7
  232.1 3.3 copy-start.119
  279.4 39.8 %copy-start.69 = (f32[8,3,384]{2,1,0:T(4,128)S(1)}, f32[8,3,384]{2,1,0:T(4,128)}, u32[]{:S(2)}) copy-start(f32[8,3,384]{2,1,0:T(4,128)} %dot_general.197) | copy-start | bytes 110596
  319.5 51.4 %copy-start.99 = (f32[1,8,3]{1,2,0:T(4,128)}, f32[1,8,3]{1,2,0:T(4,128)S(1)}, u32[]{:S(2)}) copy-start(f32[1,8,3]{1,2,0:T(4,128)S(1)} %copy.721) | copy-start | bytes 292
  321.0 7.9 %copy-start.73 = (pred[8]{0:T(512)(128)(4,1)S(1)}, pred[8]{0:T(512)(128)(4,1)}, u32[]{:S(2)}) copy-start(pred[8]{0:T(512)(128)(4,1)} %copy-done.71) | copy-start | bytes 28
  323.1 99.3 %all-gather.16.cloned.1.call-start = ((), (), s32[]{:S(2)}) async-start(), calls=%async_computation.4 | async-start | bytes 1671168 | tf_op jit(solution)/shard_map/all_gather | solution.py:74
  323.3 4.9 collective-permute-start.8
  326.6 3.2 copy-start.116
  326.6 5.7 copy-start.79
  326.6 5.0 collective-permute-start.9
  329.5 3.7 copy-start.120
  368.7 3.7 copy-start.125
  379.4 118.0 %all-gather.18.cloned.1.call-start = ((), (), s32[]{:S(2)}) async-start(), calls=%async_computation.5 | async-start | bytes 1671168 | tf_op jit(solution)/shard_map/all_gather | solution.py:74
  379.5 7.5 %copy-start.74 = (pred[8]{0:T(512)(128)(4,1)S(1)}, pred[8]{0:T(512)(128)(4,1)}, u32[]{:S(2)}) copy-start(pred[8]{0:T(512)(128)(4,1)} %copy-done.71) | copy-start | bytes 28
  379.5 6.2 %collective-permute-start.10 = (f32[3,8,256]{2,1,0:T(8,128)S(1)}, f32[3,8,256]{2,1,0:T(8,128)S(1)}, u32[]{:S(2)}, u32[]{:S(2)}) collective-permute-start(f32[3,8,256]{2,1,0:T(8,128)S(1)} %bitcast.936), channel_id=1, source_target_pairs={{0,16},{16,32},{32,48},{48,64},{64,80},{80,96},{96,112},{1,17},{17... | collective-permute-start | bytes 73736 | tf_op jit(solution)/shard_map/ppermute | solution.py:20
  384.2 8.6 %collective-permute-start.11 = (f32[3,8,256]{2,1,0:T(8,128)}, f32[3,8,256]{2,1,0:T(8,128)}, u32[]{:S(2)}, u32[]{:S(2)}) collective-permute-start(f32[3,8,256]{2,1,0:T(8,128)} %bitcast.754), channel_id=1, source_target_pairs={{16,0},{32,16},{48,32},{64,48},{80,64},{96,80},{112,96},{17,1},{33... | collective-permute-start | bytes 73736 | tf_op jit(solution)/shard_map/ppermute | solution.py:20
  454.2 114.3 %all-gather.20.cloned.1.call-start = ((), (), s32[]{:S(2)}) async-start(), calls=%async_computation.6 | async-start | bytes 1671168 | tf_op jit(solution)/shard_map/all_gather | solution.py:74
  454.3 7.7 %copy-start.75 = (pred[8]{0:T(512)(128)(4,1)S(1)}, pred[8]{0:T(512)(128)(4,1)}, u32[]{:S(2)}) copy-start(pred[8]{0:T(512)(128)(4,1)} %copy-done.71) | copy-start | bytes 28
  454.3 6.4 %collective-permute-start.12 = (f32[3,8,256]{2,1,0:T(8,128)S(1)}, f32[3,8,256]{2,1,0:T(8,128)S(1)}, u32[]{:S(2)}, u32[]{:S(2)}) collective-permute-start(f32[3,8,256]{2,1,0:T(8,128)S(1)} %bitcast.937), channel_id=1, source_target_pairs={{0,16},{16,32},{32,48},{48,64},{64,80},{80,96},{96,112},{1,17},{17... | collective-permute-start | bytes 73736 | tf_op jit(solution)/shard_map/ppermute | solution.py:20
  459.2 8.7 %collective-permute-start.13 = (f32[3,8,256]{2,1,0:T(8,128)}, f32[3,8,256]{2,1,0:T(8,128)}, u32[]{:S(2)}, u32[]{:S(2)}) collective-permute-start(f32[3,8,256]{2,1,0:T(8,128)} %bitcast.752), channel_id=1, source_target_pairs={{16,0},{32,16},{48,32},{64,48},{80,64},{96,80},{112,96},{17,1},{33... | collective-permute-start | bytes 73736 | tf_op jit(solution)/shard_map/ppermute | solution.py:20
  526.1 7.5 %collective-permute-start.14 = (f32[3,8,256]{2,1,0:T(8,128)}, f32[3,8,256]{2,1,0:T(8,128)}, u32[]{:S(2)}, u32[]{:S(2)}) collective-permute-start(f32[3,8,256]{2,1,0:T(8,128)} %bitcast.751), channel_id=1, source_target_pairs={{0,16},{16,32},{32,48},{48,64},{64,80},{80,96},{96,112},{1,17},{17... | collective-permute-start | bytes 73736 | tf_op jit(solution)/shard_map/ppermute | solution.py:20
  528.5 6.5 %collective-permute-start.15 = (f32[3,8,256]{2,1,0:T(8,128)}, f32[3,8,256]{2,1,0:T(8,128)}, u32[]{:S(2)}, u32[]{:S(2)}) collective-permute-start(f32[3,8,256]{2,1,0:T(8,128)} %bitcast.750), channel_id=1, source_target_pairs={{16,0},{32,16},{48,32},{64,48},{80,64},{96,80},{112,96},{17,1},{33... | collective-permute-start | bytes 73736 | tf_op jit(solution)/shard_map/ppermute | solution.py:20
  530.9 5.6 copy-start.76
  531.0 5.6 copy-start.80
  531.8 9.1 %copy-start.121 = (pred[8]{0:T(512)(128)(4,1)S(1)}, pred[8]{0:T(512)(128)(4,1)}, u32[]{:S(2)}) copy-start(pred[8]{0:T(512)(128)(4,1)} %copy-done.118) | copy-start | bytes 28
  538.9 7.0 %copy-start.117 = (pred[8]{0:T(512)(128)(4,1)S(1)}, pred[8]{0:T(512)(128)(4,1)}, u32[]{:S(2)}) copy-start(pred[8]{0:T(512)(128)(4,1)} %copy-done.114) | copy-start | bytes 28
  584.4 8.3 %copy-start.104 = (pred[8]{0:T(512)(128)(4,1)S(1)}, pred[8]{0:T(512)(128)(4,1)}, u32[]{:S(2)}) copy-start(pred[8]{0:T(512)(128)(4,1)} %copy-done.102) | copy-start | bytes 28
  584.4 8.3 %copy-start.107 = (pred[8]{0:T(512)(128)(4,1)S(1)}, pred[8]{0:T(512)(128)(4,1)}, u32[]{:S(2)}) copy-start(pred[8]{0:T(512)(128)(4,1)} %copy-done.105) | copy-start | bytes 28
  584.4 8.3 %copy-start.110 = (pred[8]{0:T(512)(128)(4,1)S(1)}, pred[8]{0:T(512)(128)(4,1)}, u32[]{:S(2)}) copy-start(pred[8]{0:T(512)(128)(4,1)} %copy-done.108) | copy-start | bytes 28
  584.4 8.3 %copy-start.113 = (pred[8]{0:T(512)(128)(4,1)S(1)}, pred[8]{0:T(512)(128)(4,1)}, u32[]{:S(2)}) copy-start(pred[8]{0:T(512)(128)(4,1)} %copy-done.111) | copy-start | bytes 28
  593.6 3.9 copy-start.126
  (105 other events, 156.7 us)
Sparse Core Ops, SparseCore 0:
  49.8 46.6 all-gather.7
  123.5 42.9 all-gather.9
  221.5 42.9 all-gather.11
  323.3 39.9 all-gather.13
  379.5 42.9 all-gather.15
  454.3 42.9 all-gather.17
  525.5 42.9 all-gather.19
where the time goes:
time: 620 us; the launch traced here: 607 us
  local copies, waits for them, and re-layouts  207 us (33%)
  waiting for transfers between devices  160 us (26%)
  other arithmetic  92.3 us (15%)
  blocking collectives  62.9 us (10%)
  matrix products  41.7 us (7%)
  starting transfers between devices  23.6 us (4%)
  between operations  19.2 us (3%)
    all_gather x7, waiting for transfers between devices, near_faces(): gathered = lax.all_gather(face_rows, 'mem', axis=0, tiled=True)  158 us
    reduce_sum x48, other arithmetic, coarsen(): average = jnp.mean(squares, axis=(-3, -1), keepdims=True)  42 us
    unnamed x1, blocking collectives  38.1 us
    reshape x42, local copies, waits for them, and re-layouts, coarsen(): return jnp.broadcast_to(average, squares.shape).reshape(leading + (FACE,))  35.4 us
    transpose x35, local copies, waits for them, and re-layouts, ghost_set(): ghost_rows[:, direction].transpose(1, 0, 2)  31.4 us
    dot_general x32, matrix products, beside(): jnp.einsum('cbim,lm->cbil', ghosts[direction].reshape(channels, blocks_he...  27.8 us
    all_gather x1, blocking collectives, near_faces(): gathered = lax.all_gather(face_rows, 'mem', axis=0, tiled=True)  24.8 us
    ppermute x16, starting transfers between devices, shifted_2(): return lax.ppermute(block, axis, route)  23.3 us
  transfers between devices with their start and end apart: 23, of which 9 were waited for; matrix products, arithmetic and copies ran while one was open for 20% of the time, Pallas kernels for 0%

commit v1 on v0

--- a/solution.py
+++ b/solution.py
@@ -71,7 +71,26 @@
     wanted = (face_block * 4 + opposite[None, :]).reshape(-1)
 
     def near_faces(face_rows):
-        gathered = lax.all_gather(face_rows, "mem", axis=0, tiled=True)
+        devices_2, index, rows = (lax.axis_size("mem"), lax.axis_index("mem"), face_rows.shape[0])
+        ahead = [(i_2, (i_2 + 1) % devices_2) for i_2 in range(devices_2)]
+        backward = [(i_2, (i_2 - 1) % devices_2) for i_2 in range(devices_2)]
+        whole = jnp.zeros(
+            (*face_rows.shape[:0], devices_2 * rows, *face_rows.shape[0 + 1 :]), face_rows.dtype
+        )
+        whole = lax.dynamic_update_slice_in_dim(whole, face_rows, index * rows, axis=0)
+        from_left = from_right = face_rows
+        half = devices_2 // 2
+        for lap in range(1, half + 1):
+            from_left = lax.ppermute(from_left, "mem", ahead)
+            whole = lax.dynamic_update_slice_in_dim(
+                whole, from_left, (index - lap) % devices_2 * rows, axis=0
+            )
+            if lap < devices_2 - half:
+                from_right = lax.ppermute(from_right, "mem", backward)
+                whole = lax.dynamic_update_slice_in_dim(
+                    whole, from_right, (index + lap) % devices_2 * rows, axis=0
+                )
+        gathered = whole
         return gathered[owners * (4 * blocks_here) + wanted]
 
     def ghost_set(stacked):

time: 620 us -> 943 us (1.52)
  the two profiles are of different devices: /device:TPU:0 before, /device:TPU:96 now
where the time goes in v1:
time: 943 us; the launch traced here: 927 us
  starting transfers between devices  357 us (38%)
  local copies, waits for them, and re-layouts  288 us (31%)
  waiting for transfers between devices  108 us (11%)
  other arithmetic  91.3 us (10%)
  matrix products  41.3 us (4%)
  blocking collectives  35.4 us (4%)
    ppermute x56, starting transfers between devices, near_faces(): from_right = lax.ppermute(from_right, 'mem', backward)  308 us
    ppermute x64, waiting for transfers between devices, near_faces(): from_left = lax.ppermute(from_left, 'mem', ahead)  98 us
    ppermute x16, starting transfers between devices, shifted_2(): return lax.ppermute(block, axis, route)  43.7 us
    dynamic_update_slice x64, local copies, waits for them, and re-layouts, near_faces(): lax.dynamic_update_slice_in_dim(whole, from_left, (index - lap) % devices...  41.6 us
    dynamic_update_slice x56, local copies, waits for them, and re-layouts, near_faces(): lax.dynamic_update_slice_in_dim(whole, from_right, (index + lap) % device...  35.9 us
    reduce_sum x48, other arithmetic, coarsen(): average = jnp.mean(squares, axis=(-3, -1), keepdims=True)  35.8 us
    unnamed x1, blocking collectives  35.4 us
    reshape x42, local copies, waits for them, and re-layouts, coarsen(): return jnp.broadcast_to(average, squares.shape).reshape(leading + (FACE,))  28.8 us
  transfers between devices with their start and end apart: 136, of which 76 were waited for; matrix products, arithmetic and copies ran while one was open for 22% of the time, Pallas kernels for 0%

profile of v1, /device:TPU:96, one launch (start us, length us, event | category | flops | bytes accessed | tf_op | source)
XLA Modules:
  0.0 926.7 jit_solution(15187204219219680091)
XLA Ops:
  4.7 3.9 collective-permute-start.1
  21.4 5.3 collective-permute-start.3
  28.6 5.3 collective-permute-start.5
  35.8 5.3 collective-permute-start.7
  43.0 5.3 collective-permute-start.9
  50.3 5.5 collective-permute-start.11
  57.5 5.5 collective-permute-start.13
  64.8 7.2 collective-permute-done.14
  77.9 5.8 collective-permute-start.18
  114.2 5.3 collective-permute-start.20
  122.0 5.6 collective-permute-start.22
  129.9 5.7 collective-permute-start.24
  137.8 5.7 collective-permute-start.26
  145.7 5.7 collective-permute-start.28
  154.4 5.8 collective-permute-start.30
  163.1 6.6 collective-permute-done.31
  202.6 5.3 collective-permute-start.35
  248.1 5.4 collective-permute-start.37
  255.9 5.6 collective-permute-start.39
  263.8 5.7 collective-permute-start.41
  271.7 6.0 collective-permute-start.43
  279.9 5.7 collective-permute-start.45
  288.5 5.8 collective-permute-start.47
  297.1 6.5 collective-permute-done.48
  359.2 5.3 collective-permute-start.52
  384.3 5.4 collective-permute-start.54
  392.0 5.6 collective-permute-start.56
  399.9 5.6 collective-permute-start.58
  407.8 5.6 collective-permute-start.60
  415.8 5.6 collective-permute-start.62
  424.3 5.8 collective-permute-start.64
  433.2 6.6 collective-permute-done.65
  457.1 35.4 %all-reduce = f32[384]{0:T(512)S(1)} all-reduce(f32[384]{0:T(512)S(1)} %dynamic-update-slice), channel_id=1, replica_groups=mesh['grp'=8,'mem'=16] {'mem'}, use_global_device_ids=true, to_apply=%add | all-reduce | flops 384 | bytes 3072
  516.2 5.4 collective-permute-start.71
  524.2 5.3 collective-permute-start.73
  532.1 5.4 collective-permute-start.75
  540.0 5.4 collective-permute-start.77
  548.0 5.5 collective-permute-start.79
  556.9 5.3 collective-permute-start.81
  566.1 6.6 collective-permute-done.82
  589.4 5.3 collective-permute-start.86
  624.2 5.4 collective-permute-start.88
  632.1 5.6 collective-permute-start.90
  639.9 5.7 collective-permute-start.92
  647.9 6.1 collective-permute-start.94
  656.2 5.7 collective-permute-start.96
  664.8 5.8 collective-permute-start.98
  673.4 6.4 collective-permute-done.99
  712.0 5.3 collective-permute-start.103
  747.8 5.4 collective-permute-start.105
  755.7 5.6 collective-permute-start.107
  763.5 5.7 collective-permute-start.109
  771.4 5.7 collective-permute-start.111
  779.4 5.7 collective-permute-start.113
  787.8 5.8 collective-permute-start.115
  796.9 6.6 collective-permute-done.116
  832.7 5.3 collective-permute-start.120
  854.2 5.3 collective-permute-start.122
  862.1 5.6 collective-permute-start.124
  869.9 5.7 collective-permute-start.126
  877.8 5.7 collective-permute-start.128
  885.8 5.7 collective-permute-start.130
  894.4 5.8 collective-permute-start.132
  903.1 6.6 collective-permute-done.133
  (1180 shorter events, 527.0 us)
Async XLA Ops:
  3.2 18.1 %collective-permute-start = (f32[32,256]{1,0:T(8,128)S(1)}, f32[32,256]{1,0:T(8,128)S(1)}, u32[]{:S(2)}, u32[]{:S(2)}) collective-permute-start(f32[32,256]{1,0:T(8,128)S(1)} %reshape.1007), channel_id=1, source_target_pairs={{0,1},{1,2},{2,3},{3,4},{4,5},{5,6},{6,7},{7,8},{8,9},{9,10},{10,1... | collective-permute-start | bytes 98312 | tf_op jit(solution)/shard_map/ppermute | solution.py:84
  4.7 16.6 %collective-permute-start.1 = (f32[32,256]{1,0:T(8,128)S(1)}, f32[32,256]{1,0:T(8,128)S(1)}, u32[]{:S(2)}, u32[]{:S(2)}) collective-permute-start(f32[32,256]{1,0:T(8,128)S(1)} %reshape.1007), channel_id=1, source_target_pairs={{0,15},{1,0},{2,1},{3,2},{4,3},{5,4},{6,5},{7,6},{8,7},{9,8},{10,9... | collective-permute-start | bytes 98312 | tf_op jit(solution)/shard_map/ppermute | solution.py:89
  9.6 9.3 %collective-permute-start.15 = (f32[1,8,256]{2,0,1:T(1,128)S(1)}, f32[1,8,256]{2,0,1:T(1,128)S(1)}, u32[]{:S(2)}, u32[]{:S(2)}) collective-permute-start(f32[1,8,256]{2,0,1:T(1,128)S(1)} %get-tuple-element.104), channel_id=1, source_target_pairs={{0,16},{16,32},{32,48},{48,64},{64,80},{80,96},{96,112},{1,17},{17... | collective-permute-start | bytes 24584 | tf_op jit(solution)/shard_map/ppermute | solution.py:20
  11.5 8.0 collective-permute-start.16
  77.9 34.7 %collective-permute-start.17 = (f32[32,768]{1,0:T(8,128)}, f32[32,768]{1,0:T(8,128)}, u32[]{:S(2)}, u32[]{:S(2)}) collective-permute-start(f32[32,768]{1,0:T(8,128)} %reshape.1012), channel_id=1, source_target_pairs={{0,1},{1,2},{2,3},{3,4},{4,5},{5,6},{6,7},{7,8},{8,9},{9,10},{10,1... | collective-permute-start | bytes 294920 | tf_op jit(solution)/shard_map/ppermute | solution.py:84
  77.9 36.2 %collective-permute-start.18 = (f32[32,768]{1,0:T(8,128)}, f32[32,768]{1,0:T(8,128)}, u32[]{:S(2)}, u32[]{:S(2)}) collective-permute-start(f32[32,768]{1,0:T(8,128)} %reshape.1012), channel_id=1, source_target_pairs={{0,15},{1,0},{2,1},{3,2},{4,3},{5,4},{6,5},{7,6},{8,7},{9,8},{10,9... | collective-permute-start | bytes 294920 | tf_op jit(solution)/shard_map/ppermute | solution.py:89
  86.6 8.9 collective-permute-start.32
  91.9 10.8 %collective-permute-start.33 = (f32[3,8,256]{2,1,0:T(8,128)}, f32[3,8,256]{2,1,0:T(8,128)}, u32[]{:S(2)}, u32[]{:S(2)}) collective-permute-start(f32[3,8,256]{2,1,0:T(8,128)} %bitcast.764), channel_id=1, source_target_pairs={{16,0},{32,16},{48,32},{64,48},{80,64},{96,80},{112,96},{17,1},{33... | collective-permute-start | bytes 73736 | tf_op jit(solution)/shard_map/ppermute | solution.py:20
  112.6 8.5 collective-permute-start.19
  145.7 8.6 collective-permute-start.28
  152.8 8.8 collective-permute-start.29
  154.4 8.1 collective-permute-start.30
  161.6 8.1 collective-permute-start.31
  202.6 43.9 %collective-permute-start.34 = (f32[32,768]{1,0:T(8,128)}, f32[32,768]{1,0:T(8,128)}, u32[]{:S(2)}, u32[]{:S(2)}) collective-permute-start(f32[32,768]{1,0:T(8,128)} %reshape.1031), channel_id=1, source_target_pairs={{0,1},{1,2},{2,3},{3,4},{4,5},{5,6},{6,7},{7,8},{8,9},{9,10},{10,1... | collective-permute-start | bytes 294920 | tf_op jit(solution)/shard_map/ppermute | solution.py:84
  202.6 45.4 %collective-permute-start.35 = (f32[32,768]{1,0:T(8,128)}, f32[32,768]{1,0:T(8,128)}, u32[]{:S(2)}, u32[]{:S(2)}) collective-permute-start(f32[32,768]{1,0:T(8,128)} %reshape.1031), channel_id=1, source_target_pairs={{0,15},{1,0},{2,1},{3,2},{4,3},{5,4},{6,5},{7,6},{8,7},{9,8},{10,9... | collective-permute-start | bytes 294920 | tf_op jit(solution)/shard_map/ppermute | solution.py:89
  209.9 9.0 collective-permute-start.49
  215.2 16.4 %collective-permute-start.50 = (f32[3,8,256]{2,1,0:T(8,128)}, f32[3,8,256]{2,1,0:T(8,128)}, u32[]{:S(2)}, u32[]{:S(2)}) collective-permute-start(f32[3,8,256]{2,1,0:T(8,128)} %bitcast.762), channel_id=1, source_target_pairs={{16,0},{32,16},{48,32},{64,48},{80,64},{96,80},{112,96},{17,1},{33... | collective-permute-start | bytes 73736 | tf_op jit(solution)/shard_map/ppermute | solution.py:20
  246.5 8.5 collective-permute-start.36
  271.7 8.2 collective-permute-start.43
  279.9 8.6 collective-permute-start.45
  286.7 9.0 collective-permute-start.46
  288.5 8.0 collective-permute-start.47
  359.2 23.5 %collective-permute-start.51 = (f32[32,768]{1,0:T(8,128)}, f32[32,768]{1,0:T(8,128)}, u32[]{:S(2)}, u32[]{:S(2)}) collective-permute-start(f32[32,768]{1,0:T(8,128)} %reshape.1050), channel_id=1, source_target_pairs={{0,1},{1,2},{2,3},{3,4},{4,5},{5,6},{6,7},{7,8},{8,9},{9,10},{10,1... | collective-permute-start | bytes 294920 | tf_op jit(solution)/shard_map/ppermute | solution.py:84
  359.2 25.1 %collective-permute-start.52 = (f32[32,768]{1,0:T(8,128)}, f32[32,768]{1,0:T(8,128)S(1)}, u32[]{:S(2)}, u32[]{:S(2)}) collective-permute-start(f32[32,768]{1,0:T(8,128)} %reshape.1050), channel_id=1, source_target_pairs={{0,15},{1,0},{2,1},{3,2},{4,3},{5,4},{6,5},{7,6},{8,7},{9,8},{10,9... | collective-permute-start | bytes 294920 | tf_op jit(solution)/shard_map/ppermute | solution.py:89
  367.5 8.1 collective-permute-start.66
  382.7 8.1 collective-permute-start.53
  390.8 8.4 collective-permute-start.55
  407.8 8.0 collective-permute-start.60
  415.1 8.4 collective-permute-start.61
  415.8 8.5 collective-permute-start.62
  423.5 8.4 collective-permute-start.63
  424.3 8.3 collective-permute-start.64
  495.7 19.8 %collective-permute-start.68 = (f32[32,768]{1,0:T(8,128)S(1)}, f32[32,768]{1,0:T(8,128)S(1)}, u32[]{:S(2)}, u32[]{:S(2)}) collective-permute-start(f32[32,768]{1,0:T(8,128)S(1)} %reshape.1069), channel_id=1, source_target_pairs={{0,1},{1,2},{2,3},{3,4},{4,5},{5,6},{6,7},{7,8},{8,9},{9,10},{10,1... | collective-permute-start | bytes 294920 | tf_op jit(solution)/shard_map/ppermute | solution.py:84
  497.8 18.4 %collective-permute-start.69 = (f32[32,768]{1,0:T(8,128)S(1)}, f32[32,768]{1,0:T(8,128)S(1)}, u32[]{:S(2)}, u32[]{:S(2)}) collective-permute-start(f32[32,768]{1,0:T(8,128)S(1)} %reshape.1069), channel_id=1, source_target_pairs={{0,15},{1,0},{2,1},{3,2},{4,3},{5,4},{6,5},{7,6},{8,7},{9,8},{10,9... | collective-permute-start | bytes 294920 | tf_op jit(solution)/shard_map/ppermute | solution.py:89
  547.3 9.0 collective-permute-start.78
  548.0 9.0 collective-permute-start.79
  556.3 8.3 collective-permute-start.80
  556.9 8.5 collective-permute-start.81
  564.6 8.1 collective-permute-start.82
  589.4 33.2 %collective-permute-start.85 = (f32[32,768]{1,0:T(8,128)}, f32[32,768]{1,0:T(8,128)}, u32[]{:S(2)}, u32[]{:S(2)}) collective-permute-start(f32[32,768]{1,0:T(8,128)} %reshape.1088), channel_id=1, source_target_pairs={{0,1},{1,2},{2,3},{3,4},{4,5},{5,6},{6,7},{7,8},{8,9},{9,10},{10,1... | collective-permute-start | bytes 294920 | tf_op jit(solution)/shard_map/ppermute | solution.py:84
  589.4 34.8 %collective-permute-start.86 = (f32[32,768]{1,0:T(8,128)}, f32[32,768]{1,0:T(8,128)}, u32[]{:S(2)}, u32[]{:S(2)}) collective-permute-start(f32[32,768]{1,0:T(8,128)} %reshape.1088), channel_id=1, source_target_pairs={{0,15},{1,0},{2,1},{3,2},{4,3},{5,4},{6,5},{7,6},{8,7},{9,8},{10,9... | collective-permute-start | bytes 294920 | tf_op jit(solution)/shard_map/ppermute | solution.py:89
  597.6 8.1 collective-permute-start.100
  602.0 10.8 %collective-permute-start.101 = (f32[3,8,256]{2,1,0:T(8,128)}, f32[3,8,256]{2,1,0:T(8,128)}, u32[]{:S(2)}, u32[]{:S(2)}) collective-permute-start(f32[3,8,256]{2,1,0:T(8,128)} %bitcast.758), channel_id=1, source_target_pairs={{16,0},{32,16},{48,32},{64,48},{80,64},{96,80},{112,96},{17,1},{33... | collective-permute-start | bytes 73736 | tf_op jit(solution)/shard_map/ppermute | solution.py:20
  622.6 8.5 collective-permute-start.87
  647.9 8.3 collective-permute-start.94
  656.2 8.6 collective-permute-start.96
  662.9 9.0 collective-permute-start.97
  664.8 8.0 collective-permute-start.98
  711.9 34.2 %collective-permute-start.102 = (f32[32,768]{1,0:T(8,128)}, f32[32,768]{1,0:T(8,128)}, u32[]{:S(2)}, u32[]{:S(2)}) collective-permute-start(f32[32,768]{1,0:T(8,128)} %reshape.1107), channel_id=1, source_target_pairs={{0,1},{1,2},{2,3},{3,4},{4,5},{5,6},{6,7},{7,8},{8,9},{9,10},{10,1... | collective-permute-start | bytes 294920 | tf_op jit(solution)/shard_map/ppermute | solution.py:84
  712.0 35.8 %collective-permute-start.103 = (f32[32,768]{1,0:T(8,128)}, f32[32,768]{1,0:T(8,128)}, u32[]{:S(2)}, u32[]{:S(2)}) collective-permute-start(f32[32,768]{1,0:T(8,128)} %reshape.1107), channel_id=1, source_target_pairs={{0,15},{1,0},{2,1},{3,2},{4,3},{5,4},{6,5},{7,6},{8,7},{9,8},{10,9... | collective-permute-start | bytes 294920 | tf_op jit(solution)/shard_map/ppermute | solution.py:89
  720.2 8.9 collective-permute-start.117
  725.5 10.8 %collective-permute-start.118 = (f32[3,8,256]{2,1,0:T(8,128)}, f32[3,8,256]{2,1,0:T(8,128)}, u32[]{:S(2)}, u32[]{:S(2)}) collective-permute-start(f32[3,8,256]{2,1,0:T(8,128)} %bitcast.756), channel_id=1, source_target_pairs={{16,0},{32,16},{48,32},{64,48},{80,64},{96,80},{112,96},{17,1},{33... | collective-permute-start | bytes 73736 | tf_op jit(solution)/shard_map/ppermute | solution.py:20
  746.2 8.5 collective-permute-start.104
  754.7 8.1 collective-permute-start.106
  779.4 8.4 collective-permute-start.113
  786.6 9.0 collective-permute-start.114
  787.8 8.5 collective-permute-start.115
  832.7 19.9 %collective-permute-start.119 = (f32[32,768]{1,0:T(8,128)}, f32[32,768]{1,0:T(8,128)}, u32[]{:S(2)}, u32[]{:S(2)}) collective-permute-start(f32[32,768]{1,0:T(8,128)} %reshape.1127), channel_id=1, source_target_pairs={{0,1},{1,2},{2,3},{3,4},{4,5},{5,6},{6,7},{7,8},{8,9},{9,10},{10,1... | collective-permute-start | bytes 294920 | tf_op jit(solution)/shard_map/ppermute | solution.py:84
  832.7 21.5 %collective-permute-start.120 = (f32[32,768]{1,0:T(8,128)}, f32[32,768]{1,0:T(8,128)}, u32[]{:S(2)}, u32[]{:S(2)}) collective-permute-start(f32[32,768]{1,0:T(8,128)} %reshape.1127), channel_id=1, source_target_pairs={{0,15},{1,0},{2,1},{3,2},{4,3},{5,4},{6,5},{7,6},{8,7},{9,8},{10,9... | collective-permute-start | bytes 294920 | tf_op jit(solution)/shard_map/ppermute | solution.py:89
  839.9 8.2 collective-permute-start.135
  852.6 8.5 collective-permute-start.121
  885.8 8.6 collective-permute-start.130
  892.9 8.9 collective-permute-start.131
  894.4 8.1 collective-permute-start.132
  (215 other events, 1668.8 us)
